TPU v7x, 32 devices: a whole 2x2x4 slice. The times are simulated.
32 devices in a mesh: rows: 8 (over z, y), sub: 4 (over x, core).
Axes of the slice: x: 2, y: 2, z: 4, core: 2. Of those that a mesh axis runs over, the one named last changes fastest.
Arguments:
- embeddings: bfloat16 [16384, 768], P(('rows', 'sub')), may hold values from -0.25 to 0.25
- factor: float32 [16384, 512], P(('rows', 'sub')), may hold values from -0.15 to 0.15
- diagonal: float32 [16384], P(('rows', 'sub')), may hold values from 0.5 to 1
- pivot_owner: int32 [4, 256], replicated, may hold values from 0 to 31, as said below
- pivot_local: int32 [4, 256], replicated, may hold values from 0 to 511, as said below
Outputs:
- new_columns: float32 [16384, 1024], P(('rows', 'sub'))
- new_diagonal: float32 [16384], P(('rows', 'sub'))
Inputs may be any that keep to these rules, and one draw needn't show every extreme that they name: The 1024 global rows pivot_owner * 512 + pivot_local are all different; row 0 and the last row of all are among them. `pivot_local`: read together with pivot_owner.
All inputs are finite; a program needn't handle non-finite values.
Results may differ from a plain program's by a relative error of at most 0.0003.
Values sent between devices are 32-bit elements; how exact they have to be, the bound alone decides.
No kernel may reach another device: no remote copies, remote signals or barrier semaphores. Data moves between devices by JAX's collectives and lax.ppermute only.
A program may use at most 64 MiB of HBM per device.

v0:
```python
import jax
import jax.numpy as jnp
from jax import lax
from jax.sharding import PartitionSpec as P

gamma_scale = 1.0
ridge_base = 0.5


def gauss_kernel(left, left_squares, right, right_squares):
    inner = jnp.dot(left, right.T, preferred_element_type=jnp.float32)
    return jnp.exp(-gamma_scale * (left_squares[:, None] + right_squares[None, :] - 2.0 * inner))


def gershgorin(pivot_gram):
    absolute = jnp.sum(jnp.abs(pivot_gram), axis=1) - jnp.abs(jnp.diagonal(pivot_gram))
    return ridge_base + jnp.maximum(jnp.max(absolute - jnp.diagonal(pivot_gram)), 0.0)


def selector(owners, locals_row, device, local_rows):
    positions = lax.broadcasted_iota(jnp.int32, (owners.shape[0], local_rows), 1)
    hits = (owners[:, None] == device) & (locals_row[:, None] == positions)
    return hits.astype(jnp.float32)


def on_device(embeddings, factor, diagonal, pivot_owner, pivot_local):
    local_rows = embeddings.shape[0]
    pivots = pivot_owner.shape[1]
    blocks = pivot_owner.shape[0]
    device = lax.axis_index("rows") * lax.axis_size("sub") + lax.axis_index("sub")
    squares = jnp.sum(jnp.square(embeddings.astype(jnp.float32)), axis=1)
    identity = jnp.eye(pivots, dtype=jnp.float32)
    columns = factor
    residual_diag = diagonal
    blocks_out = []
    later_rows = [[] for block in range(blocks)]
    select_all = selector(pivot_owner.reshape(-1), pivot_local.reshape(-1), device, local_rows)
    all_points = jnp.dot(
        select_all.astype(jnp.bfloat16), embeddings, preferred_element_type=jnp.float32
    )
    all_factor = jnp.dot(select_all, factor, precision=lax.Precision.HIGHEST)
    all_points, all_factor = lax.psum((all_points, all_factor), ("rows", "sub"))
    for block in range(blocks):
        point_rows = all_points[block * pivots : (block + 1) * pivots]
        factor_rows = jnp.concatenate(
            [all_factor[block * pivots : (block + 1) * pivots]] + later_rows[block], axis=1
        )
        points = point_rows.astype(jnp.bfloat16)
        point_squares = jnp.sum(point_rows * point_rows, axis=1)
        kernel = gauss_kernel(embeddings, squares, points, point_squares)
        resid = kernel - jnp.dot(columns, factor_rows.T, precision=lax.Precision.HIGHEST)
        pivot_kernel = gauss_kernel(points, point_squares, points, point_squares)
        pivot_gram = pivot_kernel - jnp.dot(
            factor_rows, factor_rows.T, precision=lax.Precision.HIGHEST
        )
        pivot_gram = 0.5 * (pivot_gram + pivot_gram.T)
        shift = gershgorin(pivot_gram)
        lower = jnp.linalg.cholesky(pivot_gram + shift * identity)
        inverse = lax.linalg.triangular_solve(lower, identity, left_side=True, lower=True)
        block_cols = jnp.dot(resid, inverse.T, precision=lax.Precision.HIGHEST)
        residual_diag = residual_diag - jnp.sum(block_cols * block_cols, axis=1)
        columns = jnp.concatenate([columns, block_cols], axis=1)
        blocks_out.append(block_cols)
        for later in range(block + 1, blocks):
            later_rows_f = all_points[later * pivots : (later + 1) * pivots]
            later_points = later_rows_f.astype(jnp.bfloat16)
            later_squares = jnp.sum(later_rows_f * later_rows_f, axis=1)
            later_cols = jnp.concatenate(
                [all_factor[later * pivots : (later + 1) * pivots]] + later_rows[later], axis=1
            )
            cross = gauss_kernel(later_points, later_squares, points, point_squares)
            cross = cross - jnp.dot(later_cols, factor_rows.T, precision=lax.Precision.HIGHEST)
            later_rows[later].append(jnp.dot(cross, inverse.T, precision=lax.Precision.HIGHEST))
    return (jnp.concatenate(blocks_out, axis=1), residual_diag)


def solution(mesh):
    return jax.shard_map(
        on_device,
        mesh=mesh,
        in_specs=(P(("rows", "sub"), None), P(("rows", "sub"), None), P(("rows", "sub")), P(), P()),
        out_specs=(P(("rows", "sub"), None), P(("rows", "sub"))),
        check_vma=False,
    )
```

profile of v0, /device:TPU:0, one launch (start us, length us, event | category | flops | bytes accessed | tf_op | source)
XLA Modules:
  0.0 617.7 jit_solution(4231253984314557761)
XLA Ops:
  8.6 3.9 fusion.62
  12.6 3.4 fusion.15
  17.6 149.4 %all-reduce.4.cloned.1.call-done = (f32[1024,768]{1,0:T(8,128)}, f32[1024,512]{1,0:T(8,128)}) async-done(((f32[1024,768]{1,0:T(8,128)}, f32[1024,512]{1,0:T(8,128)}), (f32[1024,768]{1,0:T(8,128)}, f32[1024,512]{1,0:T(8,128)})) %all-reduce.4.cloned.1.call-update) | async-done | bytes 5242896 | tf_op jit(solution)/shard_map/psum | solution.py:42
  167.0 2.1 fusion.184
  183.8 1.8 copy.72
  186.4 1.9 abs_reduce_fusion.3
  188.3 3.1 gather_fusion
  194.2 1.8 copy.78
  197.8 11.7 %cholesky.214 = f32[128,128]{1,0:T(8,128)S(1)} custom-call(f32[128,128]{1,0:T(8,128)S(1)} %copy.79), custom_call_target="Cholesky" | custom-call | tf_op jit(solution)/shard_map/jit(cholesky)/cholesky | solution.py:58
  212.1 11.3 %custom-call.25 = f32[1,128,128]{1,2,0:T(8,128)} custom-call(f32[1,128,128]{2,1,0:T(8,128)} %get-tuple-element.114), custom_call_target="InvertDiagBlocksLowerTriangular" | custom-call | tf_op jit(solution)/shard_map/jit(cholesky)/cholesky | solution.py:58
  224.5 1.7 convolution_subtract_fusion.12
  227.8 13.2 %cholesky.231 = f32[128,128]{1,0:T(8,128)} custom-call(f32[128,128]{1,0:T(8,128)} %copy.81), custom_call_target="Cholesky" | custom-call | tf_op jit(solution)/shard_map/jit(cholesky)/cholesky | solution.py:58
  247.4 6.6 %while.8 = (s32[]{:T(128)}, f32[256,256]{1,0:T(8,128)S(1)}, s32[2,2]{1,0:T(2,128)}, f32[2,128,128]{2,1,0:T(8,128)}, s32[]{:T(128)}) while((s32[]{:T(128)}, f32[256,256]{1,0:T(8,128)S(1)}, s32[2,2]{1,0:T(2,128)}, f32[2,128,128]{2,1,0:T(8,128)}, s32[]{:T(128)}) %tuple.103), condition=%wide.while_cond, body=%wide.while_body.sunk | while | flops 2 | bytes 132705 | solution.py:59
  248.8 2.0 bitcast_dynamic-update-slice_fusion.8
  252.1 2.0 bitcast_dynamic-update-slice_fusion.8
  254.0 21.3 %custom-call.26 = f32[2,128,128]{1,2,0:T(8,128)} custom-call(f32[2,128,128]{2,1,0:T(8,128)} %get-tuple-element.30), custom_call_target="InvertDiagBlocksLowerTriangular" | custom-call | tf_op jit(solution)/shard_map/triangular_solve/custom-call.0 | solution.py:59
  278.0 1.6 convolution_subtract_fusion.2
  283.3 1.8 copy.88
  285.1 1.8 copy.86
  286.9 2.0 abs_reduce_fusion.2
  289.0 3.3 gather_fusion.1
  295.0 1.8 copy.91
  298.6 11.7 %cholesky.248 = f32[128,128]{1,0:T(8,128)S(1)} custom-call(f32[128,128]{1,0:T(8,128)S(1)} %copy.92), custom_call_target="Cholesky" | custom-call | tf_op jit(solution)/shard_map/jit(cholesky)/cholesky | solution.py:58
  313.0 11.3 %custom-call.27 = f32[1,128,128]{1,2,0:T(8,128)} custom-call(f32[1,128,128]{2,1,0:T(8,128)} %get-tuple-element.110), custom_call_target="InvertDiagBlocksLowerTriangular" | custom-call | tf_op jit(solution)/shard_map/jit(cholesky)/cholesky | solution.py:58
  325.4 1.7 convolution_subtract_fusion.11
  328.7 13.2 %cholesky.265 = f32[128,128]{1,0:T(8,128)} custom-call(f32[128,128]{1,0:T(8,128)} %copy.94), custom_call_target="Cholesky" | custom-call | tf_op jit(solution)/shard_map/jit(cholesky)/cholesky | solution.py:58
  347.5 8.5 %while.9 = (s32[]{:T(128)}, f32[256,256]{1,0:T(8,128)}, s32[2,2]{1,0:T(2,128)}, f32[2,128,128]{2,1,0:T(8,128)}, s32[]{:T(128)}) while((s32[]{:T(128)}, f32[256,256]{1,0:T(8,128)}, s32[2,2]{1,0:T(2,128)}, f32[2,128,128]{2,1,0:T(8,128)}, s32[]{:T(128)}) %tuple.118), condition=%wide.while_cond.clone, body=%wide.while_body.clone.sunk | while | flops 2 | bytes 132705 | solution.py:59
  348.9 2.9 bitcast_dynamic-update-slice_fusion.9
  353.2 2.9 bitcast_dynamic-update-slice_fusion.9
  356.0 21.2 %custom-call.28 = f32[2,128,128]{1,2,0:T(8,128)} custom-call(f32[2,128,128]{2,1,0:T(8,128)} %get-tuple-element.31), custom_call_target="InvertDiagBlocksLowerTriangular" | custom-call | tf_op jit(solution)/shard_map/triangular_solve/custom-call.0 | solution.py:59
  380.9 1.6 convolution_subtract_fusion.3
  385.6 1.8 fusion.80
  389.5 1.8 copy.105
  392.1 2.0 fusion.99
  394.2 1.8 copy.106
  397.5 3.3 gather_fusion.2
  406.2 11.7 %cholesky.282 = f32[128,128]{1,0:T(8,128)S(1)} custom-call(f32[128,128]{1,0:T(8,128)S(1)} %cholesky.352), custom_call_target="Cholesky" | custom-call | tf_op jit(solution)/shard_map/jit(cholesky)/cholesky | solution.py:58
  420.5 11.3 %custom-call.29 = f32[1,128,128]{1,2,0:T(8,128)} custom-call(f32[1,128,128]{2,1,0:T(8,128)} %get-tuple-element.106), custom_call_target="InvertDiagBlocksLowerTriangular" | custom-call | tf_op jit(solution)/shard_map/jit(cholesky)/cholesky | solution.py:58
  432.9 1.7 convolution_subtract_fusion.10
  434.6 13.2 %cholesky.299 = f32[128,128]{1,0:T(8,128)} custom-call(f32[128,128]{1,0:T(8,128)} %convolution_subtract_fusion.10), custom_call_target="Cholesky" | custom-call | tf_op jit(solution)/shard_map/jit(cholesky)/cholesky | solution.py:58
  453.4 6.3 %while.10 = (s32[]{:T(128)}, f32[256,256]{1,0:T(8,128)S(1)}, s32[2,2]{1,0:T(2,128)}, f32[2,128,128]{2,1,0:T(8,128)}, s32[]{:T(128)}) while((s32[]{:T(128)}, f32[256,256]{1,0:T(8,128)S(1)}, s32[2,2]{1,0:T(2,128)}, f32[2,128,128]{2,1,0:T(8,128)}, s32[]{:T(128)}) %tuple.119), condition=%wide.while_cond.clone.1, body=%wide.while_body.clone.1.sunk | while | flops 2 | bytes 132705 | solution.py:59
  454.7 1.9 bitcast_dynamic-update-slice_fusion.10
  457.8 1.9 bitcast_dynamic-update-slice_fusion.10
  459.7 21.1 %custom-call.30 = f32[2,128,128]{1,2,0:T(8,128)} custom-call(f32[2,128,128]{2,1,0:T(8,128)} %get-tuple-element.32), custom_call_target="InvertDiagBlocksLowerTriangular" | custom-call | tf_op jit(solution)/shard_map/triangular_solve/custom-call.0 | solution.py:59
  486.2 3.5 fusion.79
  489.6 1.8 copy.124
  491.4 1.8 copy.123
  494.1 1.9 abs_reduce_fusion
  496.0 3.1 gather_fusion.3
  505.3 11.7 %cholesky.316 = f32[128,128]{1,0:T(8,128)S(1)} custom-call(f32[128,128]{1,0:T(8,128)S(1)} %cholesky.355), custom_call_target="Cholesky" | custom-call | tf_op jit(solution)/shard_map/jit(cholesky)/cholesky | solution.py:58
  519.1 11.3 %custom-call.31 = f32[1,128,128]{1,2,0:T(8,128)} custom-call(f32[1,128,128]{2,1,0:T(8,128)} %get-tuple-element.102), custom_call_target="InvertDiagBlocksLowerTriangular" | custom-call | tf_op jit(solution)/shard_map/jit(cholesky)/cholesky | solution.py:58
  531.5 1.7 convolution_subtract_fusion.9
  533.2 13.2 %cholesky.333 = f32[128,128]{1,0:T(8,128)} custom-call(f32[128,128]{1,0:T(8,128)} %convolution_subtract_fusion.9), custom_call_target="Cholesky" | custom-call | tf_op jit(solution)/shard_map/jit(cholesky)/cholesky | solution.py:58
  551.2 8.3 %while.11 = (s32[]{:T(128)}, f32[256,256]{1,0:T(8,128)}, s32[2,2]{1,0:T(2,128)}, f32[2,128,128]{2,1,0:T(8,128)}, s32[]{:T(128)}) while((s32[]{:T(128)}, f32[256,256]{1,0:T(8,128)}, s32[2,2]{1,0:T(2,128)}, f32[2,128,128]{2,1,0:T(8,128)}, s32[]{:T(128)}) %tuple.120), condition=%wide.while_cond.clone.2, body=%wide.while_body.clone.2.sunk | while | flops 2 | bytes 132705 | solution.py:59
  552.5 2.9 bitcast_dynamic-update-slice_fusion.11
  556.7 2.8 bitcast_dynamic-update-slice_fusion.11
  559.5 21.3 %custom-call.32 = f32[2,128,128]{1,2,0:T(8,128)} custom-call(f32[2,128,128]{2,1,0:T(8,128)} %get-tuple-element.33), custom_call_target="InvertDiagBlocksLowerTriangular" | custom-call | tf_op jit(solution)/shard_map/triangular_solve/custom-call.0 | solution.py:59
  583.1 1.8 fusion.136
  584.9 2.4 fusion.40
  588.9 2.1 copy.82
  591.0 2.5 fusion.17
  595.7 3.4 fusion.37
  601.3 4.0 fusion
  608.2 1.8 copy.128
  (254 shorter events, 117.1 us)
Async XLA Ops:
  7.2 159.8 %all-reduce.4.cloned.1.call-start = ((), (), s32[]{:S(2)}) async-start(), calls=%async_computation | async-start | bytes 10485760 | tf_op jit(solution)/shard_map/psum | solution.py:42
  8.6 3.9 copy-start.1
  16.0 1.4 copy-start.4
  167.0 2.8 copy-start.3
  169.8 5.8 copy-start.10
  169.8 10.2 %copy-start.12 = (bf16[256,768]{1,0:T(8,128)(2,1)}, bf16[256,768]{1,0:T(8,128)(2,1)S(1)}, u32[]{:S(2)}) copy-start(bf16[256,768]{1,0:T(8,128)(2,1)S(1)} %get-tuple-element.93) | copy-start | bytes 1179652
  170.1 9.9 %copy-start.57 = (f32[256]{0:T(256)}, f32[256]{0:T(256)S(1)}, u32[]{:S(2)}) copy-start(f32[256]{0:T(256)S(1)} %get-tuple-element.39) | copy-start | bytes 3076
  170.4 12.0 %copy-start.25 = (f32[256,256]{0,1:T(8,128)}, f32[256,256]{0,1:T(8,128)S(1)}, u32[]{:S(2)}) copy-start(f32[256,256]{0,1:T(8,128)S(1)} %convolution_multiply_fusion.13) | copy-start | bytes 786436
  175.6 3.2 copy-start.5
  178.8 2.4 copy-start
  197.0 0.7 copy-start.44
  209.5 0.6 copy-start.50
  241.9 2.6 copy-start.37
  275.3 4.3 copy-start.54
  276.5 4.8 copy-start.14
  278.0 3.8 copy-start.21
  281.8 3.4 copy-start.7
  297.8 0.7 copy-start.45
  310.3 0.6 copy-start.51
  347.5 35.4 %copy-start.8 = (f32[256,256]{1,0:T(8,128)S(1)}, f32[256,256]{1,0:T(8,128)}, u32[]{:S(2)}) copy-start(f32[256,256]{1,0:T(8,128)} %copy-done.7) | copy-start | bytes 786436
  377.3 5.2 copy-start.15
  377.3 5.2 copy-start.22
  377.3 5.7 copy-start.31
  377.3 5.7 copy-start.40
  377.3 5.7 copy-start.55
  378.5 6.6 %copy-start.19 = (f32[128,256]{1,0:T(8,128)}, f32[128,256]{1,0:T(8,128)S(1)}, u32[]{:S(2)}) copy-start(f32[128,256]{1,0:T(8,128)S(1)} %fusion.131) | copy-start | bytes 393220
  380.9 4.3 copy-start.28
  382.5 1.8 copy-start.32
  382.5 1.8 copy-start.56
  383.0 4.4 copy-start.41
  384.3 3.1 copy-start.47
  385.6 2.9 copy-start.48
  385.6 2.9 copy-start.13
  385.6 2.9 copy-start.58
  387.4 3.9 copy-start.24
  405.5 0.7 copy-start.42
  417.9 0.6 copy-start.52
  448.7 3.1 copy-start.38
  481.9 1.4 copy-start.26
  483.4 0.7 copy-start.35
  484.0 9.2 %copy-start.39 = (f32[256,256]{1,0:T(8,128)S(1)}, f32[256,256]{1,0:T(8,128)}, u32[]{:S(2)}) copy-start(f32[256,256]{1,0:T(8,128)} %get-tuple-element.116) | copy-start | bytes 786436
  485.5 0.7 copy-start.49
  504.6 0.7 copy-start.43
  517.0 0.6 copy-start.53
  551.2 36.2 %copy-start.16 = (f32[128,256]{1,0:T(8,128)S(1)}, f32[128,256]{1,0:T(8,128)}, u32[]{:S(2)}) copy-start(f32[128,256]{1,0:T(8,128)} %copy-done.14) | copy-start | bytes 393220
  551.2 36.2 %copy-start.23 = (f32[128,256]{1,0:T(8,128)S(1)}, f32[128,256]{1,0:T(8,128)}, u32[]{:S(2)}) copy-start(f32[128,256]{1,0:T(8,128)} %copy-done.21) | copy-start | bytes 393220
  582.0 1.2 copy-start.33
  584.9 6.1 copy-start.9
  587.4 3.6 copy-start.2
  588.9 4.7 copy-start.6
  588.9 4.7 copy-start.11
  591.0 3.0 copy-start.20
  591.0 3.0 copy-start.29
  593.6 2.1 copy-start.30
  595.7 3.4 copy-start.27
  595.7 3.4 copy-start.36
  600.4 5.0 copy-start.18
  605.4 0.9 copy-start.34
  605.4 1.0 copy-start.46
  605.4 1.6 copy-start.17
  608.2 1.8 copy-start.59
  608.2 1.8 copy-start.60
Sparse Core Ops, SparseCore 0:
  16.1 150.8 all-reduce.3
where the time goes:
time: 627 us; the launch traced here: 618 us
  other arithmetic  273 us (44%)
  waiting for transfers between devices  149 us (24%)
  local copies, waits for them, and re-layouts  92.4 us (15%)
  matrix products  79.7 us (13%)
  between operations  22.7 us (4%)
    another operation x27, other arithmetic, on_device(): lower = jnp.linalg.cholesky(pivot_gram + shift * identity)  159 us
    psum x1, waiting for transfers between devices, on_device(): all_points, all_factor = lax.psum((all_points, all_factor), ('rows', 'sub'))  149 us
    another operation x9, other arithmetic, on_device(): lax.linalg.triangular_solve(lower, identity, left_side=True, lower=True)  88.9 us
    another operation x29, local copies, waits for them, and re-layouts, on_device(): lax.linalg.triangular_solve(lower, identity, left_side=True, lower=True)  33.5 us
    dot_general x14, matrix products, gauss_kernel(): inner = jnp.dot(left, right.T, preferred_element_type=jnp.float32)  13 us
    gather x4, local copies, waits for them, and re-layouts, gershgorin(): jnp.diagonal(pivot_gram)  12.8 us
    another operation x12, matrix products, on_device(): lax.linalg.triangular_solve(lower, identity, left_side=True, lower=True)  12.8 us
  transfers between devices with their start and end apart: 1, of which 1 were waited for; matrix products, arithmetic and copies ran while one was open for 0% of the time, Pallas kernels for 0%

commit v1 on v0

--- a/solution.py
+++ b/solution.py
@@ -1,3 +1,4 @@
+import functools
 import jax
 import jax.numpy as jnp
 from jax import lax
@@ -5,6 +6,14 @@
 
 gamma_scale = 1.0
 ridge_base = 0.5
+
+
+def register_results(shard_in, along_axis, mesh_ax):
+    block_out = lax.psum(shard_in, axis_name=along_axis)
+    return lax.psum(block_out, axis_name=mesh_ax)
+
+
+process_roads = functools.partial(register_results, along_axis="sub", mesh_ax="rows")
 
 
 def gauss_kernel(left, left_squares, right, right_squares):
@@ -39,7 +48,7 @@
         select_all.astype(jnp.bfloat16), embeddings, preferred_element_type=jnp.float32
     )
     all_factor = jnp.dot(select_all, factor, precision=lax.Precision.HIGHEST)
-    all_points, all_factor = lax.psum((all_points, all_factor), ("rows", "sub"))
+    all_points, all_factor = process_roads((all_points, all_factor))
     for block in range(blocks):
         point_rows = all_points[block * pivots : (block + 1) * pivots]
         factor_rows = jnp.concatenate(

time: 627 us -> 771 us (1.23)
  waiting for transfers between devices: 149 us -> 292 us
    psum x1 -> x2, waiting for transfers between devices: 149 us -> 291 us  [the longest x1 186 us: register_results(): return lax.psum(block_out, axis_name=mesh_ax)]
  transfers between devices with their start and end apart: 1 -> 2, of which waited for: 1 -> 2; matrix products, arithmetic and copies ran while one was open for 0% -> 0% of each run, Pallas kernels for 0% -> 0%
where the time goes in v1:
time: 771 us; the launch traced here: 762 us
  waiting for transfers between devices  292 us (38%)
  other arithmetic  273 us (35%)
  local copies, waits for them, and re-layouts  92.7 us (12%)
  matrix products  81.4 us (11%)
  between operations  23 us (3%)
    psum x1, waiting for transfers between devices, register_results(): return lax.psum(block_out, axis_name=mesh_ax)  186 us
    another operation x27, other arithmetic, on_device(): lower = jnp.linalg.cholesky(pivot_gram + shift * identity)  159 us
    psum x1, waiting for transfers between devices, register_results(): block_out = lax.psum(shard_in, axis_name=along_axis)  105 us
    another operation x9, other arithmetic, on_device(): lax.linalg.triangular_solve(lower, identity, left_side=True, lower=True)  88.9 us
    another operation x29, local copies, waits for them, and re-layouts, on_device(): lax.linalg.triangular_solve(lower, identity, left_side=True, lower=True)  34 us
  transfers between devices with their start and end apart: 2, of which 2 were waited for; matrix products, arithmetic and copies ran while one was open for 0% of the time, Pallas kernels for 0%

profile of v1, /device:TPU:0, one launch (start us, length us, event | category | flops | bytes accessed | tf_op | source)
XLA Modules:
  0.0 761.7 jit_solution(14886337381846163552)
XLA Ops:
  8.6 3.9 fusion.62
  12.6 3.4 fusion.15
  16.0 105.4 %all-reduce.8.cloned.1.call-done = (f32[1024,768]{1,0:T(8,128)}, f32[1024,512]{1,0:T(8,128)}) async-done(((f32[1024,768]{1,0:T(8,128)}, f32[1024,512]{1,0:T(8,128)}), (f32[1024,768]{1,0:T(8,128)}, f32[1024,512]{1,0:T(8,128)})) %all-reduce.8.cloned.1.call-update) | async-done | bytes 5242896 | tf_op jit(solution)/shard_map/psum | solution.py:12
  123.0 186.1 %all-reduce.6.cloned.1.call-done = (f32[1024,768]{1,0:T(8,128)}, f32[1024,512]{1,0:T(8,128)}) async-done(((f32[1024,768]{1,0:T(8,128)}, f32[1024,512]{1,0:T(8,128)}), (f32[1024,768]{1,0:T(8,128)}, f32[1024,512]{1,0:T(8,128)})) %all-reduce.6.cloned.1.call-update) | async-done | bytes 5242896 | tf_op jit(solution)/shard_map/psum | solution.py:13
  309.2 2.1 fusion.184
  326.0 1.8 copy.72
  328.6 1.9 abs_reduce_fusion.3
  330.5 3.1 gather_fusion
  336.4 1.8 copy.78
  340.0 11.7 %cholesky.214 = f32[128,128]{1,0:T(8,128)S(1)} custom-call(f32[128,128]{1,0:T(8,128)S(1)} %copy.79), custom_call_target="Cholesky" | custom-call | tf_op jit(solution)/shard_map/jit(cholesky)/cholesky | solution.py:67
  354.3 11.3 %custom-call.25 = f32[1,128,128]{1,2,0:T(8,128)} custom-call(f32[1,128,128]{2,1,0:T(8,128)} %get-tuple-element.116), custom_call_target="InvertDiagBlocksLowerTriangular" | custom-call | tf_op jit(solution)/shard_map/jit(cholesky)/cholesky | solution.py:67
  366.8 1.7 convolution_subtract_fusion.12
  370.1 13.2 %cholesky.231 = f32[128,128]{1,0:T(8,128)} custom-call(f32[128,128]{1,0:T(8,128)} %copy.81), custom_call_target="Cholesky" | custom-call | tf_op jit(solution)/shard_map/jit(cholesky)/cholesky | solution.py:67
  389.7 6.5 while.8
  391.0 2.0 bitcast_dynamic-update-slice_fusion.8
  394.2 2.0 bitcast_dynamic-update-slice_fusion.8
  396.2 21.3 %custom-call.26 = f32[2,128,128]{1,2,0:T(8,128)} custom-call(f32[2,128,128]{2,1,0:T(8,128)} %get-tuple-element.30), custom_call_target="InvertDiagBlocksLowerTriangular" | custom-call | tf_op jit(solution)/shard_map/triangular_solve/custom-call.0 | solution.py:68
  420.1 1.6 convolution_subtract_fusion.2
  426.2 1.8 copy.88
  428.8 2.0 abs_reduce_fusion.2
  430.8 3.3 gather_fusion.1
  436.8 1.8 copy.91
  440.4 11.7 %cholesky.248 = f32[128,128]{1,0:T(8,128)S(1)} custom-call(f32[128,128]{1,0:T(8,128)S(1)} %copy.92), custom_call_target="Cholesky" | custom-call | tf_op jit(solution)/shard_map/jit(cholesky)/cholesky | solution.py:67
  454.8 11.3 %custom-call.27 = f32[1,128,128]{1,2,0:T(8,128)} custom-call(f32[1,128,128]{2,1,0:T(8,128)} %get-tuple-element.112), custom_call_target="InvertDiagBlocksLowerTriangular" | custom-call | tf_op jit(solution)/shard_map/jit(cholesky)/cholesky | solution.py:67
  467.3 1.7 convolution_subtract_fusion.11
  470.6 13.2 %cholesky.265 = f32[128,128]{1,0:T(8,128)} custom-call(f32[128,128]{1,0:T(8,128)} %copy.94), custom_call_target="Cholesky" | custom-call | tf_op jit(solution)/shard_map/jit(cholesky)/cholesky | solution.py:67
  489.5 8.6 %while.9 = (s32[]{:T(128)}, f32[256,256]{1,0:T(8,128)}, s32[2,2]{1,0:T(2,128)}, f32[2,128,128]{2,1,0:T(8,128)}, s32[]{:T(128)}) while((s32[]{:T(128)}, f32[256,256]{1,0:T(8,128)}, s32[2,2]{1,0:T(2,128)}, f32[2,128,128]{2,1,0:T(8,128)}, s32[]{:T(128)}) %tuple.121), condition=%wide.while_cond.clone, body=%wide.while_body.clone.sunk | while | flops 2 | bytes 132705 | solution.py:68
  490.9 3.0 bitcast_dynamic-update-slice_fusion.9
  495.2 2.9 bitcast_dynamic-update-slice_fusion.9
  498.2 21.3 %custom-call.28 = f32[2,128,128]{1,2,0:T(8,128)} custom-call(f32[2,128,128]{2,1,0:T(8,128)} %get-tuple-element.31), custom_call_target="InvertDiagBlocksLowerTriangular" | custom-call | tf_op jit(solution)/shard_map/triangular_solve/custom-call.0 | solution.py:68
  527.8 1.8 fusion.80
  531.6 1.8 copy.105
  534.3 2.0 fusion.99
  536.3 1.8 copy.106
  539.7 3.3 gather_fusion.2
  548.5 11.7 %cholesky.282 = f32[128,128]{1,0:T(8,128)S(1)} custom-call(f32[128,128]{1,0:T(8,128)S(1)} %cholesky.352), custom_call_target="Cholesky" | custom-call | tf_op jit(solution)/shard_map/jit(cholesky)/cholesky | solution.py:67
  562.9 11.3 %custom-call.29 = f32[1,128,128]{1,2,0:T(8,128)} custom-call(f32[1,128,128]{2,1,0:T(8,128)} %get-tuple-element.108), custom_call_target="InvertDiagBlocksLowerTriangular" | custom-call | tf_op jit(solution)/shard_map/jit(cholesky)/cholesky | solution.py:67
  575.2 1.7 convolution_subtract_fusion.10
  577.0 13.2 %cholesky.299 = f32[128,128]{1,0:T(8,128)} custom-call(f32[128,128]{1,0:T(8,128)} %convolution_subtract_fusion.10), custom_call_target="Cholesky" | custom-call | tf_op jit(solution)/shard_map/jit(cholesky)/cholesky | solution.py:67
  595.9 6.5 while.10
  597.2 2.0 bitcast_dynamic-update-slice_fusion.10
  600.4 1.9 bitcast_dynamic-update-slice_fusion.10
  602.4 21.1 %custom-call.30 = f32[2,128,128]{1,2,0:T(8,128)} custom-call(f32[2,128,128]{2,1,0:T(8,128)} %get-tuple-element.32), custom_call_target="InvertDiagBlocksLowerTriangular" | custom-call | tf_op jit(solution)/shard_map/triangular_solve/custom-call.0 | solution.py:68
  628.9 3.5 fusion.79
  632.4 1.8 copy.124
  634.1 1.8 copy.123
  636.8 1.9 abs_reduce_fusion
  638.7 3.1 gather_fusion.3
  648.1 11.7 %cholesky.316 = f32[128,128]{1,0:T(8,128)S(1)} custom-call(f32[128,128]{1,0:T(8,128)S(1)} %cholesky.355), custom_call_target="Cholesky" | custom-call | tf_op jit(solution)/shard_map/jit(cholesky)/cholesky | solution.py:67
  661.9 11.3 %custom-call.31 = f32[1,128,128]{1,2,0:T(8,128)} custom-call(f32[1,128,128]{2,1,0:T(8,128)} %get-tuple-element.104), custom_call_target="InvertDiagBlocksLowerTriangular" | custom-call | tf_op jit(solution)/shard_map/jit(cholesky)/cholesky | solution.py:67
  674.3 1.7 convolution_subtract_fusion.9
  676.0 13.2 %cholesky.333 = f32[128,128]{1,0:T(8,128)} custom-call(f32[128,128]{1,0:T(8,128)} %convolution_subtract_fusion.9), custom_call_target="Cholesky" | custom-call | tf_op jit(solution)/shard_map/jit(cholesky)/cholesky | solution.py:67
  694.2 8.4 %while.11 = (s32[]{:T(128)}, f32[256,256]{1,0:T(8,128)}, s32[2,2]{1,0:T(2,128)}, f32[2,128,128]{2,1,0:T(8,128)}, s32[]{:T(128)}) while((s32[]{:T(128)}, f32[256,256]{1,0:T(8,128)}, s32[2,2]{1,0:T(2,128)}, f32[2,128,128]{2,1,0:T(8,128)}, s32[]{:T(128)}) %tuple.123), condition=%wide.while_cond.clone.2, body=%wide.while_body.clone.2.sunk | while | flops 2 | bytes 132705 | solution.py:68
  695.6 2.9 bitcast_dynamic-update-slice_fusion.11
  699.8 2.8 bitcast_dynamic-update-slice_fusion.11
  702.7 21.3 %custom-call.32 = f32[2,128,128]{1,2,0:T(8,128)} custom-call(f32[2,128,128]{2,1,0:T(8,128)} %get-tuple-element.33), custom_call_target="InvertDiagBlocksLowerTriangular" | custom-call | tf_op jit(solution)/shard_map/triangular_solve/custom-call.0 | solution.py:68
  726.3 1.8 fusion.136
  728.1 2.5 fusion.40
  732.1 2.1 copy.82
  734.2 2.5 fusion.17
  739.9 3.5 fusion.37
  743.4 2.0 multiply_reduce_fusion.6
  746.7 3.7 fusion
  752.3 1.8 copy.128
  (265 shorter events, 119.9 us)
Async XLA Ops:
  7.2 114.2 %all-reduce.8.cloned.1.call-start = ((), (), s32[]{:S(2)}) async-start(), calls=%async_computation.1 | async-start | bytes 10485760 | tf_op jit(solution)/shard_map/psum | solution.py:12
  8.6 3.9 copy-start.1
  16.0 293.2 %all-reduce.6.cloned.1.call-start = ((), (), s32[]{:S(2)}) async-start(), calls=%async_computation | async-start | bytes 10485760 | tf_op jit(solution)/shard_map/psum | solution.py:13
  121.4 1.4 copy-start.4
  309.2 2.8 copy-start.3
  312.0 5.9 copy-start.10
  312.0 10.3 %copy-start.11 = (bf16[256,768]{1,0:T(8,128)(2,1)}, bf16[256,768]{1,0:T(8,128)(2,1)S(1)}, u32[]{:S(2)}) copy-start(bf16[256,768]{1,0:T(8,128)(2,1)S(1)} %get-tuple-element.95) | copy-start | bytes 1179652
  312.3 10.0 %copy-start.61 = (f32[256]{0:T(256)}, f32[256]{0:T(256)S(1)}, u32[]{:S(2)}) copy-start(f32[256]{0:T(256)S(1)} %get-tuple-element.39) | copy-start | bytes 3076
  312.6 12.0 %copy-start.27 = (f32[256,256]{0,1:T(8,128)}, f32[256,256]{0,1:T(8,128)S(1)}, u32[]{:S(2)}) copy-start(f32[256,256]{0,1:T(8,128)S(1)} %convolution_multiply_fusion.13) | copy-start | bytes 786436
  317.9 3.2 copy-start.5
  321.1 2.4 copy-start
  339.2 0.7 copy-start.47
  384.1 2.6 copy-start.38
  417.5 4.3 copy-start.58
  418.7 4.8 copy-start.13
  420.1 3.8 copy-start.22
  421.8 6.2 copy-start.26
  424.0 0.7 copy-start.7
  439.6 0.7 copy-start.48
  489.5 35.6 %copy-start.8 = (f32[256,256]{1,0:T(8,128)S(1)}, f32[256,256]{1,0:T(8,128)}, u32[]{:S(2)}) copy-start(f32[256,256]{1,0:T(8,128)} %copy-done.7) | copy-start | bytes 786436
  519.4 5.2 copy-start.14
  519.4 5.2 copy-start.23
  519.4 5.7 copy-start.32
  519.4 5.7 copy-start.41
  519.4 5.7 copy-start.59
  520.7 6.6 copy-start.20
  523.0 4.3 copy-start.30
  524.7 1.8 copy-start.33
  524.7 1.8 copy-start.60
  525.1 4.4 copy-start.43
  526.4 3.1 copy-start.50
  527.7 2.8 copy-start.52
  527.7 2.8 copy-start.12
  527.7 2.8 copy-start.62
  529.5 3.9 copy-start.25
  547.8 0.7 copy-start.45
  591.0 3.2 copy-start.39
  624.6 1.4 copy-start.28
  626.1 0.7 copy-start.36
  626.7 9.2 %copy-start.40 = (f32[256,256]{1,0:T(8,128)S(1)}, f32[256,256]{1,0:T(8,128)}, u32[]{:S(2)}) copy-start(f32[256,256]{1,0:T(8,128)} %get-tuple-element.118) | copy-start | bytes 786436
  628.2 0.7 copy-start.53
  647.4 0.7 copy-start.46
  659.8 0.6 copy-start.57
  694.2 36.4 %copy-start.15 = (f32[128,256]{1,0:T(8,128)S(1)}, f32[128,256]{1,0:T(8,128)}, u32[]{:S(2)}) copy-start(f32[128,256]{1,0:T(8,128)} %copy-done.13) | copy-start | bytes 393220
  694.2 36.4 %copy-start.24 = (f32[128,256]{1,0:T(8,128)S(1)}, f32[128,256]{1,0:T(8,128)}, u32[]{:S(2)}) copy-start(f32[128,256]{1,0:T(8,128)} %copy-done.22) | copy-start | bytes 393220
  725.1 1.2 copy-start.34
  728.1 6.1 copy-start.9
  730.6 3.6 copy-start.2
  732.1 4.6 copy-start.6
  734.2 4.0 copy-start.21
  734.2 4.0 copy-start.31
  736.7 3.2 copy-start.44
  738.9 4.5 copy-start.17
  739.9 3.5 copy-start.29
  739.9 3.5 copy-start.37
  743.4 3.3 copy-start.42
  743.4 3.3 copy-start.51
  750.4 0.9 copy-start.35
  750.4 1.0 copy-start.49
  750.4 1.6 copy-start.16
  750.4 1.6 copy-start.18
  750.5 1.6 copy-start.19
  752.2 1.8 copy-start.63
  752.3 1.8 copy-start.64
  (3 other events, 1.9 us)
Sparse Core Ops, SparseCore 0:
  16.1 105.2 all-reduce.7
  125.2 183.9 all-reduce.5
